TPU v7x, 32 devices: a whole 2x2x4 slice. The times are simulated.
32 devices in a mesh: grp: 2 (over y), seq: 4 (over z), fsdp: 2 (over x), tp: 2 (over core).
Axes of the slice: x: 2, y: 2, z: 4, core: 2. Of those that a mesh axis runs over, the one named last changes fastest.
Arguments:
- hidden: bfloat16 [4, 1024, 8192], P(('grp', 'fsdp'), 'seq', 'tp'), parts along dimension 0, may hold values from -480 to 480
- targets: int32 [4, 1024], P(('grp', 'fsdp'), 'seq'), parts along dimension 0, may hold values from 65 to 84, as said below
- perturb_sites: int32 [4, 64], P(('grp', 'fsdp')), parts along dimension 0, may hold values from 0 to 1023, as said below
- labels: int32 [4, 64], P(('grp', 'fsdp')), parts along dimension 0, may hold values from 0 to 1, as said below
- norm_gain: float32 [3, 8192], P(None, 'tp'), may hold values from 0.1 to 1.9
- feature_taps: bfloat16 [2, 3, 3, 8192], P(None, None, None, 'tp'), may hold values from -3.5 to 3.5
- short_taps: bfloat16 [7, 8192], P(None, 'tp'), may hold values from -2.5 to 2.5
- long_taps: bfloat16 [128, 8192], P(('seq', 'fsdp'), 'tp'), may hold values from -0.5 to 0.5
- head_weight: bfloat16 [512, 8192], P(('seq', 'fsdp'), 'tp'), may hold values from -80 to 80
Outputs:
- logprob: float32 [4, 1024], P(('grp', 'fsdp'), 'seq'), parts along dimension 0
- surprise: float32 [4, 64], P(('grp', 'fsdp')), parts along dimension 0
- contrast: float32 [4], P(('grp', 'fsdp')), parts along dimension 0
There are 2 independent parts, one for each index of `grp`. A program takes and returns all parts, laid end to end along the dimension named above; an argument that names none is the same for every part. Nothing has to cross between parts.
Inputs may be any that keep to these rules, and one draw needn't show every extreme that they name: `targets`: each target is the byte code of one of the nucleotides A, C, G, T: 65, 67, 71 or 84. `perturb_sites`: the positions of one genome rise, one in each of 64 equal blocks of the genome; the first is 0 and the last 1023. `labels`: exactly 32 sites of each genome are labelled 1.
All inputs are finite; a program needn't handle non-finite values.
Results may differ from a plain program's by a relative error of at most 0.001.
The roundings to bfloat16 on the way count: a program that leaves them out, or rounds other values in their place, can miss the bound.
Values may be sent and summed in bfloat16 or wider, within the bound.
A program may use at most 64 MiB of HBM per device.

v0:
```python
import jax
import jax.numpy as jnp
from jax import lax
from jax.sharding import PartitionSpec as P

D = 8192
FEAT_TAPS = 3
SE_TAPS = 7
MR_TAPS = 128
SITES = 64


eps = 1e-06


def passed_along(shard, axis, by):
    devices = lax.axis_size(axis)
    pairs = [(i, i + by) for i in range(devices) if 0 <= i + by < devices]
    return lax.ppermute(shard, axis, pairs)


def prefix(value, axis, join, neutral):
    count, mine = (lax.axis_size(axis), lax.axis_index(axis))
    pieces = lax.all_gather(value, axis)
    subtotal = jnp.full_like(value, 0) + jnp.asarray(neutral, value.dtype)

    def hop(position, subtotal):
        longer = join(subtotal, pieces[position])
        return jnp.where(position < mine, longer, subtotal)

    return lax.fori_loop(0, count - 1, hop, subtotal)


def settle(tensor):
    return lax.optimization_barrier(tensor.astype(jnp.bfloat16))


def causal_valid(signal, filter_taps):
    tap_count = filter_taps.shape[0]
    out_len = signal.shape[0] - tap_count + 1
    wide_taps = filter_taps.astype(jnp.float32)
    total = wide_taps[0] * signal[tap_count - 1 : tap_count - 1 + out_len].astype(jnp.float32)
    for lag in range(1, tap_count):
        start = tap_count - 1 - lag
        total = total + wide_taps[lag] * signal[start : start + out_len].astype(jnp.float32)
    return total


def normalize(residual, gain_row):
    widened = residual.astype(jnp.float32)
    row_power = lax.psum(jnp.sum(widened * widened, axis=1), "tp")
    scale_rows = lax.rsqrt(row_power / D + eps)
    return settle(widened * scale_rows[:, None] * gain_row)


def mixer(residual, normed_ext, feature_set, inner_taps):
    lead_rows = inner_taps.shape[0] - 1
    queries = settle(causal_valid(normed_ext[lead_rows:], feature_set[0]))
    key_part = settle(causal_valid(normed_ext, feature_set[1]))
    value_part = settle(causal_valid(normed_ext, feature_set[2]))
    inner_term = settle(key_part.astype(jnp.float32) * value_part.astype(jnp.float32))
    filtered = causal_valid(inner_term, inner_taps)
    return settle(residual.astype(jnp.float32) + queries.astype(jnp.float32) * filtered)


def add_terms(earlier_term, later_term):
    return earlier_term + later_term


def shards(
    hidden,
    targets,
    perturb_sites,
    labels,
    norm_gain,
    feature_taps,
    short_taps,
    long_taps,
    head_weight,
):
    residual = hidden[0]
    row_count = residual.shape[0]
    short_back = FEAT_TAPS + SE_TAPS - 2
    long_back = FEAT_TAPS + MR_TAPS - 2
    normed = normalize(residual, norm_gain[0])
    rim_rows = passed_along(normed[row_count - short_back :], "seq", 1)
    after_short = mixer(
        residual, jnp.concatenate([rim_rows, normed], axis=0), feature_taps[0], short_taps
    )
    normed_now = normalize(after_short, norm_gain[1])
    rim_long = passed_along(normed_now[row_count - long_back :], "seq", 1)
    normed_long = jnp.concatenate([rim_long, normed_now], axis=0)
    taps_all = lax.all_gather(long_taps, ("seq", "fsdp"), axis=0, tiled=True)
    after_long = mixer(after_short, normed_long, feature_taps[1], taps_all)
    final_norm = normalize(after_long, norm_gain[2])
    row_contract = (((1,), (1,)), ((), ()))
    logits_part = lax.dot_general(
        final_norm,
        lax.all_gather(head_weight, ("seq", "fsdp"), axis=0, tiled=True),
        row_contract,
        preferred_element_type=jnp.float32,
    )
    logits = lax.psum(logits_part, "tp")
    row_peak = jnp.max(logits, axis=1, keepdims=True)
    log_total = jnp.log(jnp.sum(jnp.exp(logits - row_peak), axis=1)) + row_peak[:, 0]
    target_row = targets[0]
    vocab_ids = lax.broadcasted_iota(jnp.int32, logits.shape, 1)
    chosen = jnp.sum(jnp.where(vocab_ids == target_row[:, None], logits, 0.0), axis=1)
    logprob = chosen - log_total
    site_row = perturb_sites[0]
    first_row = lax.axis_index("seq") * row_count
    positions = first_row + lax.broadcasted_iota(jnp.int32, (site_row.shape[0], row_count), 1)
    at_site = positions == site_row[:, None]
    site_value = jnp.sum(jnp.where(at_site, logprob[None, :], 0.0), axis=1)
    carry_in = prefix(jnp.sum(logprob), "seq", add_terms, jnp.zeros((), jnp.float32))
    running = jnp.concatenate([jnp.zeros((1,), jnp.float32), jnp.cumsum(logprob)[:-1]], axis=0)
    local_before = jnp.sum(jnp.where(at_site, running[None, :], 0.0), axis=1)
    is_owned = jnp.any(at_site, axis=1)
    before_term = jnp.where(is_owned, carry_in + local_before, 0.0)
    prefix_sum, site_logprob = lax.psum((before_term, site_value), "seq")
    prefix_len = jnp.maximum(site_row, 1).astype(jnp.float32)
    surprise = site_logprob - prefix_sum / prefix_len
    label_sign = (2 * labels[0] - 1).astype(jnp.float32)
    contrast = jnp.sum(label_sign * surprise) / (SITES // 2)
    return (logprob[None, :], surprise[None, :], jnp.reshape(contrast, (1,)))


def solution(mesh):
    placed = (
        P(("grp", "fsdp"), "seq", "tp"),
        P(("grp", "fsdp"), "seq"),
        P(("grp", "fsdp"), None),
        P(("grp", "fsdp"), None),
        P(None, "tp"),
        P(None, None, None, "tp"),
        P(None, "tp"),
        P(("seq", "fsdp"), "tp"),
        P(("seq", "fsdp"), "tp"),
    )
    return jax.shard_map(
        shards,
        mesh=mesh,
        in_specs=placed,
        out_specs=(P(("grp", "fsdp"), "seq"), P(("grp", "fsdp"), None), P(("grp", "fsdp"))),
        check_vma=False,
    )
```

profile of v0, /device:TPU:0, one launch (start us, length us, event | category | flops | bytes accessed | tf_op | source)
XLA Modules:
  0.0 302.3 jit_solution(16902483953333040546)
XLA Ops:
  7.2 1.6 fusion.42
  8.8 2.1 fusion.19
  10.9 2.6 psum.42
  13.5 2.2 fusion.21
  15.8 4.8 %collective-permute-start = (bf16[8,4096]{1,0:T(8,128)(2,1)S(1)}, bf16[8,4096]{1,0:T(8,128)(2,1)S(1)}, u32[]{:S(2)}, u32[]{:S(2)}) collective-permute-start(bf16[8,4096]{1,0:T(8,128)(2,1)S(1)} %slice.1299), channel_id=1, source_target_pairs={{0,4},{4,8},{8,12},{1,5},{5,9},{9,13},{2,6},{6,10},{10,14},{3,7},{... | collective-permute-start | bytes 196616 | tf_op jit(solution)/shard_map/ppermute | solution.py:19
  20.7 0.3 slice_convert_fusion.1
  21.1 1.4 collective-permute-done
  22.5 1.6 add_convert_fusion.1
  24.1 2.4 fusion.8
  26.5 0.8 multiply_convert_fusion.1
  27.4 0.8 copy-done.3
  28.1 4.3 %fusion.22 = bf16[256,4096]{1,0:T(8,128)(2,1)S(1)} fusion(bf16[256,4096]{1,0:T(8,128)(2,1)S(1)} %add_convert_fusion.1, bf16[262,4096]{1,0:T(8,128)(2,1)S(1)} %multiply_convert_fusion.1, bf16[1,256,4096]{2,1,0:T(8,128)(2,1)S(1)} %copy-done.3, f32[4096]{0:T(1024)S(1)} %bitcast.338, f32[4096]{0:T(1024)S(1)} %bitcast.337, f32[4096]{0:T(1024)S(1)} %bitcast.336, ...), kind=kLoop, calls=%fused_computation.52 | loop fusion | flops 26214400 | bytes 21086208 | tf_op jit(solution)/shard_map/convert_element_type | solution.py:35
  32.5 0.5 fusion.15
  33.0 2.5 psum.43
  35.4 0.7 fusion.17
  36.2 1.4 copy-done.1
  37.6 1.3 slice.1331
  38.9 4.4 %collective-permute-start.1 = (bf16[129,4096]{1,0:T(8,128)(2,1)}, bf16[129,4096]{1,0:T(8,128)(2,1)S(1)}, u32[]{:S(2)}, u32[]{:S(2)}) collective-permute-start(bf16[129,4096]{1,0:T(8,128)(2,1)} %slice.1331), channel_id=1, source_target_pairs={{0,4},{4,8},{8,12},{1,5},{5,9},{9,13},{2,6},{6,10},{10,14},{3,7},{... | collective-permute-start | bytes 3170312 | tf_op jit(solution)/shard_map/ppermute | solution.py:19
  43.5 34.5 %collective-permute-done.1 = bf16[129,4096]{1,0:T(8,128)(2,1)S(1)} collective-permute-done((bf16[129,4096]{1,0:T(8,128)(2,1)}, bf16[129,4096]{1,0:T(8,128)(2,1)S(1)}, u32[]{:S(2)}, u32[]{:S(2)}) %collective-permute-start.1) | collective-permute-done | bytes 1056800 | tf_op jit(solution)/shard_map/ppermute | solution.py:19
  78.1 5.3 %add_convert_fusion = bf16[256,4096]{1,0:T(8,128)(2,1)} fusion(bf16[256,4096]{1,0:T(8,128)(2,1)} %copy-done.1, bf16[129,4096]{1,0:T(8,128)(2,1)S(1)} %collective-permute-done.1, f32[4096]{0:T(1024)S(1)} %bitcast.312, f32[4096]{0:T(1024)S(1)} %bitcast.313, f32[4096]{0:T(1024)S(1)} %bitcast.311), kind=kLoop, calls=%fused_computation.54 | loop fusion | flops 15728640 | bytes 5300224 | tf_op jit(solution)/shard_map/convert_element_type | solution.py:35
  83.4 3.7 %fusion.2 = (bf16[383,4096]{1,0:T(8,128)(2,1)S(1)}, bf16[383,4096]{1,0:T(8,128)(2,1)S(1)}) fusion(f32[4096]{0:T(1024)S(1)} %bitcast.324, f32[4096]{0:T(1024)S(1)} %bitcast.325, f32[4096]{0:T(1024)S(1)} %bitcast.323, bf16[256,4096]{1,0:T(8,128)(2,1)S(1)} %copy-done.2, bf16[129,4096]{1,0:T(8,128)(2,1)S(1)} %collective-permute-done.1, f32[4096]{0:T(1024)S(1)} %bitcast.327, ...), kind=kLoop, calls=%fused_computation.8 | loop fusion | flops 50200576 | bytes 9527296 | tf_op jit(solution)/shard_map/convert_element_type | solution.py:35
  87.1 1.2 multiply_convert_fusion
  88.4 1.9 fusion.41
  90.3 2.5 fusion.40
  92.8 2.7 fusion.39
  95.5 2.5 fusion.38
  98.0 2.6 fusion.37
  100.7 2.5 fusion.36
  103.2 2.5 fusion.35
  105.7 123.4 %fusion.18 = bf16[256,4096]{1,0:T(8,128)(2,1)} fusion(bf16[256,4096]{1,0:T(8,128)(2,1)} %copy-done, bf16[256,4096]{1,0:T(8,128)(2,1)} %add_convert_fusion, bf16[383,4096]{1,0:T(8,128)(2,1)S(1)} %multiply_convert_fusion, f32[4096]{0:T(1024)S(1)} %bitcast.196, f32[4096]{0:T(1024)S(1)} %bitcast.195, f32[4096]{0:T(1024)S(1)} %bitcast.194, ...), kind=kLoop, calls=%fused_computation.48 | loop fusion | flops 406847488 | bytes 276824064 | tf_op jit(solution)/shard_map/convert_element_type | solution.py:35
  229.1 2.1 fusion.12
  231.1 2.7 psum.44
  233.8 2.2 fusion.14
  236.2 4.3 %fusion.50 = f32[256,512]{1,0:T(8,128)} fusion(bf16[256,4096]{1,0:T(8,128)(2,1)S(1)} %fusion.14, bf16[512,4096]{1,0:T(8,128)(2,1)} %all-gather.5.cloned.1.call-done), kind=kOutput, calls=%fused_computation.112 | convolution fusion | flops 1073741824 | bytes 6815744 | tf_op jit(solution)/shard_map/dot_general | solution.py:97
  240.5 0.7 dynamic-slice
  241.3 21.9 %all-reduce.4.cloned.1.call-done = f32[256,512]{1,0:T(8,128)} async-done(((f32[256,512]{1,0:T(8,128)}), f32[256,512]{1,0:T(8,128)}) %all-reduce.4.cloned.1.call-update) | async-done | bytes 524304 | tf_op jit(solution)/shard_map/psum | solution.py:103
  263.2 1.2 reduce_max.9
  264.4 1.3 exponential_reduce_fusion
  265.7 0.6 fusion.34
  266.4 0.3 reduce-window.9
  267.1 1.4 dynamic-update-slice
  268.6 12.0 %all-reduce = f32[4]{0:T(128)S(1)} all-reduce(f32[4]{0:T(128)S(1)} %dynamic-update-slice), channel_id=1, replica_groups=mesh['grp'=2,'seq'=4,'fsdp'=2,'tp'=2] {'seq'}, use_global_device_ids=true, to_apply=%add | all-reduce | flops 4 | bytes 32
  280.6 3.8 %while.13 = (s32[]{:T(128)}, f32[]{:T(128)}, s32[]{:T(128)}, f32[4]{0:T(128)S(1)}, s32[]{:T(128)}) while((s32[]{:T(128)}, f32[]{:T(128)}, s32[]{:T(128)}, f32[4]{0:T(128)S(1)}, s32[]{:T(128)}) %tuple.193), condition=%wide.region_15.16_spmd, body=%wide.region_14.15_spmd.sunk | while | flops 5 | bytes 115 | solution.py:31
  280.6 0.6 dynamic_slice.8
  281.9 0.6 dynamic_slice.8
  283.1 0.6 dynamic_slice.8
  284.4 8.4 %all-reduce.1 = (f32[64]{0:T(128)S(1)}, f32[64]{0:T(128)S(1)}) all-reduce(f32[64]{0:T(128)S(1)} %get-tuple-element.86, f32[64]{0:T(128)S(1)} %add_select_fusion), channel_id=1, replica_groups=mesh['grp'=2,'seq'=4,'fsdp'=2,'tp'=2] {'seq'}, use_global_device_ids=true, to_apply=%region_11.12 | all-reduce | flops 128 | bytes 1024 | tf_op jit(solution)/shard_map/psum | solution.py:120
  292.8 1.1 fusion.33
  (46 shorter events, 1.3 us)
Async XLA Ops:
  7.2 13.5 %copy-start.4 = (bf16[2,3,3,4096]{3,0,2,1:T(2,128)(2,1)S(1)}, bf16[2,3,3,4096]{3,0,2,1:T(2,128)(2,1)}, u32[]{:S(2)}) copy-start(bf16[2,3,3,4096]{3,0,2,1:T(2,128)(2,1)} %param.16) | copy-start | bytes 442372
  7.2 13.8 %copy-start.5 = (bf16[7,4096]{1,0:T(8,128)(2,1)S(1)}, bf16[7,4096]{1,0:T(8,128)(2,1)}, u32[]{:S(2)}) copy-start(bf16[7,4096]{1,0:T(8,128)(2,1)} %param.17) | copy-start | bytes 172036
  7.2 81.2 %all-gather.3.cloned.1.call-start = ((), (), s32[]{:S(2)}) async-start(), calls=%async_computation | async-start | bytes 1179648 | tf_op jit(solution)/shard_map/all_gather | solution.py:93
  15.8 6.7 %collective-permute-start = (bf16[8,4096]{1,0:T(8,128)(2,1)S(1)}, bf16[8,4096]{1,0:T(8,128)(2,1)S(1)}, u32[]{:S(2)}, u32[]{:S(2)}) collective-permute-start(bf16[8,4096]{1,0:T(8,128)(2,1)S(1)} %slice.1299), channel_id=1, source_target_pairs={{0,4},{4,8},{8,12},{1,5},{5,9},{9,13},{2,6},{6,10},{10,14},{3,7},{... | collective-permute-start | bytes 196616 | tf_op jit(solution)/shard_map/ppermute | solution.py:19
  20.6 215.5 %all-gather.5.cloned.1.call-start = ((), (), s32[]{:S(2)}) async-start(), calls=%async_computation.1 | async-start | bytes 4718592 | tf_op jit(solution)/shard_map/all_gather | solution.py:99
  26.5 1.6 copy-start.3
  32.5 6.4 %copy-start = (bf16[256,4096]{1,0:T(8,128)(2,1)}, bf16[256,4096]{1,0:T(8,128)(2,1)S(1)}, u32[]{:S(2)}) copy-start(bf16[256,4096]{1,0:T(8,128)(2,1)S(1)} %fusion.22) | copy-start | bytes 6291460
  36.2 1.4 copy-start.1
  38.9 39.2 %collective-permute-start.1 = (bf16[129,4096]{1,0:T(8,128)(2,1)}, bf16[129,4096]{1,0:T(8,128)(2,1)S(1)}, u32[]{:S(2)}, u32[]{:S(2)}) collective-permute-start(bf16[129,4096]{1,0:T(8,128)(2,1)} %slice.1331), channel_id=1, source_target_pairs={{0,4},{4,8},{8,12},{1,5},{5,9},{9,13},{2,6},{6,10},{10,14},{3,7},{... | collective-permute-start | bytes 3170312 | tf_op jit(solution)/shard_map/ppermute | solution.py:19
  43.3 40.1 %copy-start.2 = (bf16[256,4096]{1,0:T(8,128)(2,1)S(1)}, bf16[256,4096]{1,0:T(8,128)(2,1)}, u32[]{:S(2)}) copy-start(bf16[256,4096]{1,0:T(8,128)(2,1)} %copy-done.1) | copy-start | bytes 6291460
  43.3 220.0 %all-reduce.4.cloned.1.call-start = ((), (), s32[]{:S(2)}) async-start(), calls=%async_computation.2 | async-start | bytes 1048576 | tf_op jit(solution)/shard_map/psum | solution.py:103
  236.1 4.4 %copy-start.10 = (u32[32]{0:T(128)S(1)}, u32[32]{0:T(128)}, u32[]{:S(2)}) copy-start(u32[32]{0:T(128)} %constant.63) | copy-start | bytes 388
  236.1 5.0 %copy-start.7 = (s32[1,64]{1,0:T(1,128)S(1)}, s32[1,64]{1,0:T(1,128)}, u32[]{:S(2)}) copy-start(s32[1,64]{1,0:T(1,128)} %param.13) | copy-start | bytes 772
  236.1 28.3 %copy-start.8 = (s32[1,256]{1,0:T(1,128)S(1)}, s32[1,256]{1,0:T(1,128)}, u32[]{:S(2)}) copy-start(s32[1,256]{1,0:T(1,128)} %param.12) | copy-start | bytes 3076
  236.1 56.7 %copy-start.9 = (s32[1,64]{1,0:T(1,128)S(1)}, s32[1,64]{1,0:T(1,128)}, u32[]{:S(2)}) copy-start(s32[1,64]{1,0:T(1,128)} %param.14) | copy-start | bytes 772
  266.4 28.2 %copy-start.6 = (f32[256]{0:T(256)}, f32[256]{0:T(256)S(1)}, u32[]{:S(2)}) copy-start(f32[256]{0:T(256)S(1)} %get-tuple-element.100) | copy-start | bytes 3076
Sparse Core Ops, SparseCore 0:
  20.7 41.9 all-gather.2
  64.8 75.0 all-gather.4
  240.6 22.6 all-reduce.3
where the time goes:
time: 304 us; the launch traced here: 302 us
  other arithmetic  158 us (52%)
  waiting for transfers between devices  58 us (19%)
  blocking collectives  28.2 us (9%)
  local copies, waits for them, and re-layouts  26.5 us (9%)
  between operations  15.9 us (5%)
  starting transfers between devices  9.46 us (3%)
  matrix products  4.27 us (1%)
    convert_element_type x11, other arithmetic, settle(): return lax.optimization_barrier(tensor.astype(jnp.bfloat16))  148 us
    ppermute x2, waiting for transfers between devices, passed_along(): return lax.ppermute(shard, axis, pairs)  36 us
    psum x1, waiting for transfers between devices, shards(): logits = lax.psum(logits_part, 'tp')  21.9 us
    slice x6, local copies, waits for them, and re-layouts, causal_valid(): wide_taps[lag] * signal[start:start + out_len].astype(jnp.float32)  14.8 us
    unnamed x1, blocking collectives  12 us
    ppermute x2, starting transfers between devices, passed_along(): return lax.ppermute(shard, axis, pairs)  9.16 us
    psum x1, blocking collectives, shards(): prefix_sum, site_logprob = lax.psum((before_term, site_value), 'seq')  8.41 us
    psum x3, blocking collectives, normalize(): row_power = lax.psum(jnp.sum(widened * widened, axis=1), 'tp')  7.77 us
  transfers between devices with their start and end apart: 5, of which 3 were waited for; matrix products, arithmetic and copies ran while one was open for 56% of the time, Pallas kernels for 0%

commit v1 on v0

v1 whole, which is shorter than its diff:
```python
import functools

import jax
import jax.numpy as jnp
import numpy as np
from jax import lax
from jax.experimental import pallas as pl
from jax.experimental.pallas import tpu as pltpu
from jax.sharding import PartitionSpec as P

D = 8192
FEAT_TAPS = 3
SE_TAPS = 7
MR_TAPS = 128
SITES = 64


eps = 1e-06


def passed_along(shard, axis, by):
    devices = lax.axis_size(axis)
    pairs = [(i, i + by) for i in range(devices) if 0 <= i + by < devices]
    return lax.ppermute(shard, axis, pairs)


def settle(tensor):
    return lax.optimization_barrier(tensor.astype(jnp.bfloat16))


def split_parts(matrix, parts):
    pieces, left = [], np.asarray(matrix, np.float64)
    for _ in range(parts):
        piece = left.astype(jnp.bfloat16)
        pieces.append(piece)
        left = left - piece.astype(np.float64)
    return np.stack(pieces)


def transform_pair(window, taps):
    half = window // 2
    t = np.arange(window)
    f = np.arange(half)
    angle = 2.0 * np.pi * ((f[:, None] * t[None, :]) % window) / window
    cos_rows, sin_rows = np.cos(angle), np.sin(angle)
    sin_rows[0] = np.where(t % 2 == 0, 1.0, -1.0)
    forward = np.concatenate([cos_rows, sin_rows], axis=0)
    weight = np.full((half,), 2.0 / window)
    weight[0] = 1.0 / window
    inverse = (forward * np.concatenate([weight, weight])[:, None]).T[taps:]
    return split_parts(forward, PARTS), split_parts(inverse, PARTS)


PARTS = 3
CHUNK = 32
WIDTH = 256


def wide(value):
    return value.astype(jnp.float32)


def rounded(value):
    return value.astype(jnp.bfloat16).astype(jnp.float32)


def tap_sum(ref, start, rows, taps):
    total = taps[0] * ref[start : start + rows, :]
    for lag in range(1, len(taps)):
        total = total + taps[lag] * ref[start - lag : start - lag + rows, :]
    return total


def feature_rows(feat_ref, which):
    return [feat_ref[which * FEAT_TAPS + lag : which * FEAT_TAPS + lag + 1, :] for lag in range(FEAT_TAPS)]


def square_lanes(value):
    square = value * value
    total = square[:, :128]
    for at in range(128, square.shape[1], 128):
        total = total + square[:, at : at + 128]
    return total


def short_kernel(hid_ref, rim_ref, scale_ref, gain_ref, feat_ref, taps_ref, out_ref, pow_ref, ext, inner):
    rows = hid_ref.shape[0]
    lead = rim_ref.shape[0]
    tap_count = taps_ref.shape[0]

    @pl.when(pl.program_id(0) == 0)
    def _():
        pow_ref[...] = jnp.zeros_like(pow_ref)

    ext[0:lead, :] = jnp.zeros((lead, ext.shape[1]), jnp.float32)
    ext[lead : 2 * lead, :] = wide(rim_ref[...])
    gain = gain_ref[...]
    for at in range(0, rows, CHUNK):
        block = wide(hid_ref[at : at + CHUNK, :])
        ext[2 * lead + at : 2 * lead + at + CHUNK, :] = rounded(block * scale_ref[at : at + CHUNK, :] * gain)
    k_taps, v_taps = feature_rows(feat_ref, 1), feature_rows(feat_ref, 2)

    def inner_rows(at, count):
        keys = rounded(tap_sum(ext, lead + at, count, k_taps))
        values = rounded(tap_sum(ext, lead + at, count, v_taps))
        inner[at : at + count, :] = rounded(keys * values)

    inner_rows(0, lead)
    for at in range(0, rows, CHUNK):
        inner_rows(lead + at, CHUNK)
    q_taps = feature_rows(feat_ref, 0)
    short = [taps_ref[lag : lag + 1, :] for lag in range(tap_count)]
    for at in range(0, rows, CHUNK):
        queries = rounded(tap_sum(ext, 2 * lead + at, CHUNK, q_taps))
        filtered = tap_sum(inner, lead + at, CHUNK, short)
        result = (wide(hid_ref[at : at + CHUNK, :]) + queries * filtered).astype(jnp.bfloat16)
        out_ref[at : at + CHUNK, :] = result
        pow_ref[at : at + CHUNK, :] += square_lanes(wide(result))


def short_mixer(residual, rim, scale, gain_row, features, taps):
    rows, channels = residual.shape
    lead = rim.shape[0]
    column = lambda i: (0, i)
    fixed = lambda i: (0, 0)
    return pl.pallas_call(
        short_kernel,
        grid=(channels // WIDTH,),
        in_specs=[
            pl.BlockSpec((rows, WIDTH), column),
            pl.BlockSpec((lead, WIDTH), column),
            pl.BlockSpec((rows, 1), fixed),
            pl.BlockSpec((1, WIDTH), column),
            pl.BlockSpec((features.shape[0], WIDTH), column),
            pl.BlockSpec((taps.shape[0], WIDTH), column),
        ],
        out_specs=[pl.BlockSpec((rows, WIDTH), column), pl.BlockSpec((rows, 128), fixed)],
        out_shape=[
            jax.ShapeDtypeStruct((rows, channels), jnp.bfloat16),
            jax.ShapeDtypeStruct((rows, 128), jnp.float32),
        ],
        scratch_shapes=[
            pltpu.VMEM((2 * lead + rows, WIDTH), jnp.float32),
            pltpu.VMEM((lead + rows, WIDTH), jnp.float32),
        ],
        name="short_mixer",
    )(residual, rim, scale, gain_row, features, taps)


def long_kernel(
    res_ref, rim_ref, scale_ref, gain_ref, feat_ref, taps_ref, fwd_ref, inv_ref,
    out_ref, pow_ref, ext, inner, spec_u, spec_w, spec_y, filt,
):
    rows = res_ref.shape[0]
    tap_count = taps_ref.shape[0]
    lead = rim_ref.shape[0]
    window = tap_count + rows
    half = window // 2

    @pl.when(pl.program_id(0) == 0)
    def _():
        pow_ref[...] = jnp.zeros_like(pow_ref)

    ext[0:lead, :] = wide(rim_ref[...])
    gain = gain_ref[...]
    for at in range(0, rows, CHUNK):
        block = wide(res_ref[at : at + CHUNK, :])
        ext[lead + at : lead + at + CHUNK, :] = rounded(block * scale_ref[at : at + CHUNK, :] * gain)
    k_taps, v_taps = feature_rows(feat_ref, 1), feature_rows(feat_ref, 2)
    first = lead - tap_count
    for at in range(0, window, CHUNK):
        keys = rounded(tap_sum(ext, first + at, CHUNK, k_taps))
        values = rounded(tap_sum(ext, first + at, CHUNK, v_taps))
        inner[at : at + CHUNK, :] = (keys * values).astype(jnp.bfloat16)

    def product(left, right):
        return jnp.dot(left, right, preferred_element_type=jnp.float32)

    def forward_of(value, depth):
        total = product(fwd_ref[PARTS - 1][:, :depth], value)
        for part in range(PARTS - 2, -1, -1):
            total = total + product(fwd_ref[part][:, :depth], value)
        return total

    taps = taps_ref[...]
    signal = inner[...]
    spec_w[...] = forward_of(taps, tap_count)
    spec_u[...] = forward_of(signal, window)
    for at in range(0, half, CHUNK):
        lo, hi = slice(at, at + CHUNK), slice(half + at, half + at + CHUNK)
        uc, us, wc, ws = spec_u[lo, :], spec_u[hi, :], spec_w[lo, :], spec_w[hi, :]
        cc, ss = uc * wc, us * ws
        yc, ys = cc - ss, uc * ws + us * wc
        if at == 0:
            is_first = lax.broadcasted_iota(jnp.int32, cc.shape, 0) == 0
            yc, ys = jnp.where(is_first, cc, yc), jnp.where(is_first, ss, ys)
        for rows_at, value in ((lo, yc), (hi, ys)):
            for part in range(PARTS):
                top = value.astype(jnp.bfloat16)
                spec_y[part, rows_at, :] = top
                value = value - wide(top)
    total = None
    for order in range(PARTS - 1, -1, -1):
        for part in range(order + 1):
            term = product(inv_ref[part], spec_y[order - part])
            total = term if total is None else total + term
    filt[...] = total
    q_taps = feature_rows(feat_ref, 0)
    for at in range(0, rows, CHUNK):
        queries = rounded(tap_sum(ext, lead + at, CHUNK, q_taps))
        result = (wide(res_ref[at : at + CHUNK, :]) + queries * filt[at : at + CHUNK, :]).astype(jnp.bfloat16)
        out_ref[at : at + CHUNK, :] = result
        pow_ref[at : at + CHUNK, :] += square_lanes(wide(result))


def long_mixer(residual, rim, scale, gain_row, features, taps):
    rows, channels = residual.shape
    lead, tap_count = rim.shape[0], taps.shape[0]
    window = rows + tap_count
    forward, inverse = transform_pair(window, tap_count)
    column = lambda i: (0, i)
    fixed = lambda i: (0, 0)
    whole = lambda i: (0, 0, 0)
    return pl.pallas_call(
        long_kernel,
        grid=(channels // WIDTH,),
        in_specs=[
            pl.BlockSpec((rows, WIDTH), column),
            pl.BlockSpec((lead, WIDTH), column),
            pl.BlockSpec((rows, 1), fixed),
            pl.BlockSpec((1, WIDTH), column),
            pl.BlockSpec((features.shape[0], WIDTH), column),
            pl.BlockSpec((tap_count, WIDTH), column),
            pl.BlockSpec(forward.shape, whole),
            pl.BlockSpec(inverse.shape, whole),
        ],
        out_specs=[pl.BlockSpec((rows, WIDTH), column), pl.BlockSpec((rows, 128), fixed)],
        out_shape=[
            jax.ShapeDtypeStruct((rows, channels), jnp.bfloat16),
            jax.ShapeDtypeStruct((rows, 128), jnp.float32),
        ],
        scratch_shapes=[
            pltpu.VMEM((lead + rows, WIDTH), jnp.float32),
            pltpu.VMEM((window, WIDTH), jnp.bfloat16),
            pltpu.VMEM((window, WIDTH), jnp.float32),
            pltpu.VMEM((window, WIDTH), jnp.float32),
            pltpu.VMEM((PARTS, window, WIDTH), jnp.bfloat16),
            pltpu.VMEM((rows, WIDTH), jnp.float32),
        ],
        name="long_mixer",
    )(residual, rim, scale, gain_row, features, taps, jnp.asarray(forward), jnp.asarray(inverse))


def row_scale(row_power):
    other = lax.ppermute(row_power, "tp", [(0, 1), (1, 0)])
    return lax.rsqrt((row_power + other) / D + eps)


def scaled_rows(residual, scale_rows, gain_row):
    return settle(residual.astype(jnp.float32) * scale_rows[:, None] * gain_row)


def spread_kernel(count, mine_ref, all_ref, send_sem, recv_sem):
    me = lax.axis_index("seq")
    barrier = pltpu.get_barrier_semaphore()
    for step in range(1, count):
        peer = lax.rem(me + step, count)
        pl.semaphore_signal(barrier, inc=1, device_id={"seq": peer}, device_id_type=pl.DeviceIdType.MESH)
    pl.semaphore_wait(barrier, count - 1)
    copies = []
    for step in range(1, count):
        peer = lax.rem(me + step, count)
        copy = pltpu.make_async_remote_copy(
            src_ref=mine_ref,
            dst_ref=all_ref.at[me],
            send_sem=send_sem.at[step],
            recv_sem=recv_sem.at[step],
            device_id={"seq": peer},
            device_id_type=pl.DeviceIdType.MESH,
        )
        copy.start()
        copies.append(copy)
    all_ref[me] = mine_ref[...]
    for copy in copies:
        copy.wait()


def spread(value):
    count = lax.axis_size("seq")
    return pl.pallas_call(
        functools.partial(spread_kernel, count),
        out_shape=jax.ShapeDtypeStruct((count, *value.shape), value.dtype),
        in_specs=[pl.BlockSpec(memory_space=pltpu.VMEM)],
        out_specs=pl.BlockSpec(memory_space=pltpu.VMEM),
        scratch_shapes=[pltpu.SemaphoreType.DMA((count,)), pltpu.SemaphoreType.DMA((count,))],
        compiler_params=pltpu.CompilerParams(collective_id=0, has_side_effects=True),
        name="spread",
    )(value)


def shards(
    hidden,
    targets,
    perturb_sites,
    labels,
    norm_gain,
    feature_taps,
    short_taps,
    long_taps,
    head_weight,
):
    residual = hidden[0]
    row_count = residual.shape[0]
    short_back = FEAT_TAPS + SE_TAPS - 2
    long_back = FEAT_TAPS + MR_TAPS - 2
    long_lead = -(-long_back // 8) * 8
    widened = residual.astype(jnp.float32)
    scale_one = row_scale(jnp.sum(widened * widened, axis=1))
    last = row_count - short_back
    rim_rows = passed_along(scaled_rows(residual[last:], scale_one[last:], norm_gain[0]), "seq", 1)
    features = feature_taps.astype(jnp.float32).reshape(2, 3 * FEAT_TAPS, -1)
    after_short, power_two = short_mixer(
        residual, rim_rows, scale_one[:, None], norm_gain[0:1], features[0], short_taps.astype(jnp.float32)
    )
    scale_two = row_scale(jnp.sum(power_two, axis=1))
    last = row_count - long_back
    rim_long = passed_along(scaled_rows(after_short[last:], scale_two[last:], norm_gain[1]), "seq", 1)
    rim_long = jnp.pad(rim_long, ((long_lead - long_back, 0), (0, 0)))
    taps_all = lax.all_gather(long_taps, ("seq", "fsdp"), axis=0, tiled=True)
    after_long, power_three = long_mixer(
        after_short, rim_long, scale_two[:, None], norm_gain[1:2], features[1], taps_all
    )
    final_norm = scaled_rows(after_long, row_scale(jnp.sum(power_three, axis=1)), norm_gain[2])
    row_contract = (((1,), (1,)), ((), ()))
    logits_part = lax.dot_general(
        final_norm,
        lax.all_gather(head_weight, ("seq", "fsdp"), axis=0, tiled=True),
        row_contract,
        preferred_element_type=jnp.float32,
    )
    core = lax.axis_index("tp")
    swap = [(0, 1), (1, 0)]
    half_rows = row_count // 2
    kept = lax.dynamic_slice_in_dim(logits_part, core * half_rows, half_rows, 0)
    given = lax.dynamic_slice_in_dim(logits_part, (1 - core) * half_rows, half_rows, 0)
    logits = kept + lax.ppermute(given, "tp", swap)
    row_peak = jnp.max(logits, axis=1, keepdims=True)
    log_total = jnp.log(jnp.sum(jnp.exp(logits - row_peak), axis=1)) + row_peak[:, 0]
    target_row = lax.dynamic_slice_in_dim(targets[0], core * half_rows, half_rows, 0)
    vocab_ids = lax.broadcasted_iota(jnp.int32, logits.shape, 1)
    chosen = jnp.sum(jnp.where(vocab_ids == target_row[:, None], logits, 0.0), axis=1)
    mine = chosen - log_total
    theirs = lax.ppermute(mine, "tp", swap)
    logprob = jnp.where(core == 0, jnp.concatenate([mine, theirs]), jnp.concatenate([theirs, mine]))
    site_row = perturb_sites[0]
    genome_row = spread(logprob.reshape(-1, 128)).reshape(-1)
    positions = lax.broadcasted_iota(jnp.int32, (site_row.shape[0], genome_row.shape[0]), 1)
    prefix_sum = jnp.sum(jnp.where(positions < site_row[:, None], genome_row[None, :], 0.0), axis=1)
    site_logprob = jnp.sum(jnp.where(positions == site_row[:, None], genome_row[None, :], 0.0), axis=1)
    prefix_len = jnp.maximum(site_row, 1).astype(jnp.float32)
    surprise = site_logprob - prefix_sum / prefix_len
    label_sign = (2 * labels[0] - 1).astype(jnp.float32)
    contrast = jnp.sum(label_sign * surprise) / (SITES // 2)
    return (logprob[None, :], surprise[None, :], jnp.reshape(contrast, (1,)))


def solution(mesh):
    placed = (
        P(("grp", "fsdp"), "seq", "tp"),
        P(("grp", "fsdp"), "seq"),
        P(("grp", "fsdp"), None),
        P(("grp", "fsdp"), None),
        P(None, "tp"),
        P(None, None, None, "tp"),
        P(None, "tp"),
        P(("seq", "fsdp"), "tp"),
        P(("seq", "fsdp"), "tp"),
    )
    return jax.shard_map(
        shards,
        mesh=mesh,
        in_specs=placed,
        out_specs=(P(("grp", "fsdp"), "seq"), P(("grp", "fsdp"), None), P(("grp", "fsdp"))),
        check_vma=False,
    )
```

time: 304 us -> 162 us (0.53)
  other arithmetic: 158 us -> 13.3 us
  Pallas kernels: 0 us -> 59.3 us
  blocking collectives: 28.2 us -> 0 us
  local copies, waits for them, and re-layouts: 26.5 us -> 6.24 us
  waiting for transfers between devices: 58 us -> 52.9 us
    convert_element_type x11 -> x3, other arithmetic: 148 us -> 4.84 us  [settle(): return lax.optimization_barrier(tensor.astype(jnp.bfloat16))]
    pallas_call x0 -> x3, Pallas kernels: none -> 59.3 us  [the longest x1 37.1 us: long_mixer(): pl.pallas_call(long_kernel, grid=(channels // WIDTH,), in_specs=[pl.Block...]
    psum x1 -> x0, waiting for transfers between devices: 21.9 us -> none  [shards(): logits = lax.psum(logits_part, 'tp')]
    slice x15 -> x4, local copies, waits for them, and re-layouts: 20.4 us -> 1.03 us  [the longest x1 0.85 us: shards(): features[1]]
    psum x4 -> x0, blocking collectives: 16.2 us -> none  [the longest x1 8.41 us: shards(): prefix_sum, site_logprob = lax.psum((before_term, site_value), 'seq')]
    unnamed x1 -> x0, blocking collectives: 12 us -> none
    all_gather x1, waiting for transfers between devices: 0.02 us -> 11.2 us  [shards(): lax.all_gather(head_weight, ('seq', 'fsdp'), axis=0, tiled=True)]
    ppermute x0 -> x5, waiting for transfers between devices: none -> 5.45 us  [the longest x3 2.93 us: row_scale(): other = lax.ppermute(row_power, 'tp', [(0, 1), (1, 0)])]
  transfers between devices with their start and end apart: 5 -> 9, of which waited for: 3 -> 7; matrix products, arithmetic and copies ran while one was open for 56% -> 10% of each run, Pallas kernels for 0% -> 33%
where the time goes in v1:
time: 162 us; the launch traced here: 161 us
  Pallas kernels  59.3 us (37%)
  waiting for transfers between devices  52.9 us (33%)
  between operations  16.1 us (10%)
  other arithmetic  13.3 us (8%)
  starting transfers between devices  9.39 us (6%)
  local copies, waits for them, and re-layouts  6.24 us (4%)
  matrix products  3.51 us (2%)
    pallas_call x1, Pallas kernels, long_mixer(): pl.pallas_call(long_kernel, grid=(channels // WIDTH,), in_specs=[pl.Block...  37.1 us
    ppermute x2, waiting for transfers between devices, passed_along(): return lax.ppermute(shard, axis, pairs)  34.9 us
    pallas_call x1, Pallas kernels, short_mixer(): pl.pallas_call(short_kernel, grid=(channels // WIDTH,), in_specs=[pl.Bloc...  15.4 us
    all_gather x1, waiting for transfers between devices, shards(): lax.all_gather(head_weight, ('seq', 'fsdp'), axis=0, tiled=True)  11.2 us
    ppermute x2, starting transfers between devices, passed_along(): return lax.ppermute(shard, axis, pairs)  8.35 us
    pallas_call x1, Pallas kernels, spread(): pl.pallas_call(functools.partial(spread_kernel, count), out_shape=jax.Sha...  6.72 us
    convert_element_type x3, other arithmetic, settle(): return lax.optimization_barrier(tensor.astype(jnp.bfloat16))  4.84 us
    dot_general x1, matrix products, shards(): lax.dot_general(final_norm, lax.all_gather(head_weight, ('seq', 'fsdp'),...  3.51 us
  transfers between devices with their start and end apart: 9, of which 7 were waited for; matrix products, arithmetic and copies ran while one was open for 10% of the time, Pallas kernels for 33%

profile of v1, /device:TPU:0, one launch (start us, length us, event | category | flops | bytes accessed | tf_op | source)
XLA Modules:
  0.0 160.7 jit_solution(11949057487814549855)
XLA Ops:
  7.2 0.0 copy-start
  7.2 0.0 all-gather.3.cloned.1.call-start
  7.2 0.7 all-gather.3.cloned.1.call-update
  7.9 0.0 all-gather.5.cloned.1.call-start
  8.0 0.7 all-gather.5.cloned.1.call-update
  8.7 2.1 %multiply_reduce_fusion = f32[256]{0:T(256)S(1)} fusion(bf16[1,256,4096]{2,1,0:T(8,128)(2,1)} %param.11), kind=kLoop, calls=%fused_computation.1 | loop fusion | flops 3145472 | bytes 2098176 | tf_op jit(solution)/shard_map/reduce_sum | solution.py:318
  10.8 0.6 collective-permute-start
  11.4 0.1 convert_element_type.48
  11.5 0.6 collective-permute-done
  12.2 0.1 slice.33
  12.3 0.9 fusion.1
  13.2 4.8 %collective-permute-start.1 = (bf16[8,4096]{1,0:T(8,128)(2,1)S(1)}, bf16[8,4096]{1,0:T(8,128)(2,1)S(1)}, u32[]{:S(2)}, u32[]{:S(2)}) collective-permute-start(bf16[8,4096]{1,0:T(8,128)(2,1)S(1)} %fusion.1), channel_id=1, source_target_pairs={{0,4},{4,8},{8,12},{1,5},{5,9},{9,13},{2,6},{6,10},{10,14},{3,7},{... | collective-permute-start | bytes 196616 | tf_op jit(solution)/shard_map/ppermute | solution.py:24
  18.0 0.8 slice_reduce_fusion
  18.9 0.8 squeeze.13.feat_ref
  19.6 0.7 convert_element_type.49.taps_ref
  20.3 0.8 copy.16.scale_ref
  21.1 0.6 copy-done.5
  21.7 15.4 %short_mixer.1 = (bf16[256,4096]{1,0:T(8,128)(2,1)}, f32[256,128]{1,0:T(8,128)}) custom-call(bf16[256,4096]{1,0:T(8,128)(2,1)} %bitcast.32, bf16[8,4096]{1,0:T(8,128)(2,1)} %copy-done.5, f32[256,1]{1,0:T(8,128)} %copy.16.scale_ref, f32[1,4096]{1,0:T(1,128)} %copy-done.2, f32[9,4096]{1,0:T(8,128)} %squeeze.13.feat_ref, f32[7,4096]{1,0:T(8,128)} %convert_element_type.49.taps_ref), custom_call_target="tpu_custom_call" | custom-call | tf_op jit(solution)/shard_map/short_mixer/pallas_call | solution.py:126
  37.1 1.0 reduce_sum.77
  38.2 0.1 collective-permute-start.2
  38.2 1.1 collective-permute-done.2
  39.4 0.1 slice.37
  39.5 1.7 %multiply_convert_fusion.1 = bf16[129,4096]{1,0:T(8,128)(2,1)S(1)} fusion(f32[4096]{0:T(1024)S(1)} %bitcast.33, f32[129]{0:T(256)S(1)} %slice.37, bf16[256,4096]{1,0:T(8,128)(2,1)} %get-tuple-element.7.res_ref), kind=kLoop, calls=%fused_computation.2 | loop fusion | flops 2113536 | bytes 2130436 | tf_op jit(solution)/shard_map/convert_element_type | solution.py:28
  41.1 3.5 %collective-permute-start.3 = (bf16[129,4096]{1,0:T(8,128)(2,1)S(1)}, bf16[129,4096]{1,0:T(8,128)(2,1)S(1)}, u32[]{:S(2)}, u32[]{:S(2)}) collective-permute-start(bf16[129,4096]{1,0:T(8,128)(2,1)S(1)} %multiply_convert_fusion.1), channel_id=1, source_target_pairs={{0,4},{4,8},{8,12},{1,5},{5,9},{9,13},{2,6},{6,10},{10,14},{3,7},{... | collective-permute-start | bytes 3170312 | tf_op jit(solution)/shard_map/ppermute | solution.py:24
  44.7 0.8 squeeze.14.feat_ref
  45.5 0.8 copy.17.scale_ref
  46.3 34.9 %collective-permute-done.3 = bf16[129,4096]{1,0:T(8,128)(2,1)S(1)} collective-permute-done((bf16[129,4096]{1,0:T(8,128)(2,1)S(1)}, bf16[129,4096]{1,0:T(8,128)(2,1)S(1)}, u32[]{:S(2)}, u32[]{:S(2)}) %collective-permute-start.3) | collective-permute-done | bytes 1056800 | tf_op jit(solution)/shard_map/ppermute | solution.py:24
  81.2 1.4 pad.4.rim_ref
  82.5 37.1 %long_mixer.1 = (bf16[256,4096]{1,0:T(8,128)(2,1)}, f32[256,128]{1,0:T(8,128)}) custom-call(bf16[256,4096]{1,0:T(8,128)(2,1)} %get-tuple-element.7.res_ref, bf16[136,4096]{1,0:T(8,128)(2,1)} %pad.4.rim_ref, f32[256,1]{1,0:T(8,128)} %copy.17.scale_ref, f32[1,4096]{1,0:T(1,128)} %copy-done.1, f32[9,4096]{1,0:T(8,128)} %squeeze.14.feat_ref, ...), custom_call_target="tpu_custom_call" | custom-call | tf_op jit(solution)/shard_map/long_mixer/pallas_call | solution.py:224
  119.7 1.0 reduce_sum.78
  120.7 0.1 collective-permute-start.4
  120.8 1.1 collective-permute-done.4
  121.9 2.2 %multiply_convert_fusion = bf16[256,4096]{1,0:T(8,128)(2,1)S(1)} fusion(bf16[256,4096]{1,0:T(8,128)(2,1)} %get-tuple-element.9, f32[4096]{0:T(1024)S(1)} %bitcast.35, f32[256]{0:T(256)S(1)} %add_rsqrt_fusion), kind=kLoop, calls=%fused_computation | loop fusion | flops 4194304 | bytes 4211712 | tf_op jit(solution)/shard_map/convert_element_type | solution.py:28
  124.2 0.0 copy-start.7
  124.2 11.2 %all-gather.5.cloned.1.call-done = bf16[512,4096]{1,0:T(8,128)(2,1)} async-done(((bf16[64,4096]{1,0:T(8,128)(2,1)}), bf16[512,4096]{1,0:T(8,128)(2,1)}) %all-gather.5.cloned.1.call-update) | async-done | bytes 4194320 | tf_op jit(solution)/shard_map/all_gather | solution.py:337
  135.4 3.5 %fusion.8 = f32[256,512]{1,0:T(8,128)S(1)} fusion(bf16[256,4096]{1,0:T(8,128)(2,1)S(1)} %multiply_convert_fusion, bf16[512,4096]{1,0:T(8,128)(2,1)} %all-gather.5.cloned.1.call-done), kind=kOutput, calls=%fused_computation.32 | convolution fusion | flops 1073741824 | bytes 6815744 | tf_op jit(solution)/shard_map/dot_general | solution.py:335
  139.0 0.1 collective-permute-start.5
  139.1 1.5 collective-permute-done.5
  140.6 0.1 fusion.6
  140.7 0.2 exponential_reduce_fusion
  140.9 0.2 collective-permute-start.6
  141.1 1.0 collective-permute-done.6
  142.2 0.6 fusion.2.mine_ref
  142.7 6.7 %spread.1 = f32[4,2,128]{2,1,0:T(2,128)} custom-call(f32[2,128]{1,0:T(2,128)} %fusion.2.mine_ref), custom_call_target="tpu_custom_call" | custom-call | tf_op jit(solution)/shard_map/spread/pallas_call | solution.py:290
  149.5 0.9 select_reduce_fusion.1
  150.4 0.5 fusion.5
  150.9 0.6 fusion.4
  152.2 0.6 broadcast_select_fusion
  (24 shorter events, 0.1 us)
Async XLA Ops:
  7.2 131.9 %copy-start = (s32[1,256]{1,0:T(1,128)S(1)}, s32[1,256]{1,0:T(1,128)}, u32[]{:S(2)}) copy-start(s32[1,256]{1,0:T(1,128)} %param.12) | copy-start | bytes 3076
  7.2 4.2 %copy-start.6 = (f32[3,4096]{1,0:T(4,128)S(1)}, f32[3,4096]{1,0:T(4,128)}, u32[]{:S(2)}) copy-start(f32[3,4096]{1,0:T(4,128)} %param.15) | copy-start | bytes 147460
  7.2 4.2 %copy-start.3 = (bf16[2,3,3,4096]{3,0,2,1:T(2,128)(2,1)S(1)}, bf16[2,3,3,4096]{3,0,2,1:T(2,128)(2,1)}, u32[]{:S(2)}) copy-start(bf16[2,3,3,4096]{3,0,2,1:T(2,128)(2,1)} %param.16) | copy-start | bytes 442372
  7.2 75.3 %all-gather.3.cloned.1.call-start = ((), (), s32[]{:S(2)}) async-start(), calls=%async_computation | async-start | bytes 1179648 | tf_op jit(solution)/shard_map/all_gather | solution.py:329
  7.9 127.5 %all-gather.5.cloned.1.call-start = ((), (), s32[]{:S(2)}) async-start(), calls=%async_computation.1 | async-start | bytes 4718592 | tf_op jit(solution)/shard_map/all_gather | solution.py:337
  8.7 11.0 %copy-start.4 = (bf16[7,4096]{1,0:T(8,128)(2,1)S(1)}, bf16[7,4096]{1,0:T(8,128)(2,1)}, u32[]{:S(2)}) copy-start(bf16[7,4096]{1,0:T(8,128)(2,1)} %param.17) | copy-start | bytes 172036
  10.8 1.4 collective-permute-start
  11.4 9.7 %copy-start.2 = (f32[1,4096]{1,0:T(1,128)}, f32[1,4096]{1,0:T(1,128)S(1)}, u32[]{:S(2)}) copy-start(f32[1,4096]{1,0:T(1,128)S(1)} %get-tuple-element.20.gain_ref) | copy-start | bytes 49156
  11.4 28.0 %copy-start.1 = (f32[1,4096]{1,0:T(1,128)}, f32[1,4096]{1,0:T(1,128)S(1)}, u32[]{:S(2)}) copy-start(f32[1,4096]{1,0:T(1,128)S(1)} %get-tuple-element.21.gain_ref) | copy-start | bytes 49156
  13.2 7.9 %collective-permute-start.1 = (bf16[8,4096]{1,0:T(8,128)(2,1)S(1)}, bf16[8,4096]{1,0:T(8,128)(2,1)S(1)}, u32[]{:S(2)}, u32[]{:S(2)}) collective-permute-start(bf16[8,4096]{1,0:T(8,128)(2,1)S(1)} %fusion.1), channel_id=1, source_target_pairs={{0,4},{4,8},{8,12},{1,5},{5,9},{9,13},{2,6},{6,10},{10,14},{3,7},{... | collective-permute-start | bytes 196616 | tf_op jit(solution)/shard_map/ppermute | solution.py:24
  21.1 0.6 copy-start.5
  38.2 1.2 collective-permute-start.2
  41.1 40.0 %collective-permute-start.3 = (bf16[129,4096]{1,0:T(8,128)(2,1)S(1)}, bf16[129,4096]{1,0:T(8,128)(2,1)S(1)}, u32[]{:S(2)}, u32[]{:S(2)}) collective-permute-start(bf16[129,4096]{1,0:T(8,128)(2,1)S(1)} %multiply_convert_fusion.1), channel_id=1, source_target_pairs={{0,4},{4,8},{8,12},{1,5},{5,9},{9,13},{2,6},{6,10},{10,14},{3,7},{... | collective-permute-start | bytes 3170312 | tf_op jit(solution)/shard_map/ppermute | solution.py:24
  120.7 1.2 collective-permute-start.4
  124.2 25.3 %copy-start.7 = (s32[1,64]{1,0:T(1,128)S(1)}, s32[1,64]{1,0:T(1,128)}, u32[]{:S(2)}) copy-start(s32[1,64]{1,0:T(1,128)} %param.13) | copy-start | bytes 772
  124.2 26.7 %copy-start.8 = (s32[1,64]{1,0:T(1,128)S(1)}, s32[1,64]{1,0:T(1,128)}, u32[]{:S(2)}) copy-start(s32[1,64]{1,0:T(1,128)} %param.14) | copy-start | bytes 772
  139.0 1.6 collective-permute-start.5
  140.9 1.2 collective-permute-start.6
Sparse Core Ops, SparseCore 0:
  10.1 42.9 all-gather.2
  55.3 80.0 all-gather.4

commit v2 on v1

--- a/solution.py
+++ b/solution.py
@@ -71,8 +71,13 @@
     return total
 
 
+def tap_rows(taps):
+    taps = wide(taps)
+    return [taps[lag : lag + 1, :] for lag in range(taps.shape[0])]
+
+
 def feature_rows(feat_ref, which):
-    return [feat_ref[which * FEAT_TAPS + lag : which * FEAT_TAPS + lag + 1, :] for lag in range(FEAT_TAPS)]
+    return tap_rows(feat_ref[0, which])
 
 
 def square_lanes(value):
@@ -83,18 +88,65 @@
     return total
 
 
-def short_kernel(hid_ref, rim_ref, scale_ref, gain_ref, feat_ref, taps_ref, out_ref, pow_ref, ext, inner):
+def gather_peer(step, counts):
+    outer, inner = counts
+    place = lax.rem(lax.axis_index("seq") * inner + lax.axis_index("fsdp") + step, outer * inner)
+    return place, {"seq": place // inner, "fsdp": lax.rem(place, inner)}
+
+
+def short_kernel(
+    counts, hid_ref, rim_ref, scale_ref, gain_ref, feat_ref, taps_ref, piece_ref,
+    out_ref, pow_ref, whole_ref, ext, inner, send_sem, recv_sem, own_sem,
+):
     rows = hid_ref.shape[0]
     lead = rim_ref.shape[0]
-    tap_count = taps_ref.shape[0]
+    holders = counts[0] * counts[1]
+    mine, _ = gather_peer(0, counts)
+
+    def to_peer(step):
+        _, where = gather_peer(step, counts)
+        return pltpu.make_async_remote_copy(
+            src_ref=piece_ref,
+            dst_ref=whole_ref.at[mine],
+            send_sem=send_sem.at[step],
+            recv_sem=recv_sem.at[step],
+            device_id=where,
+            device_id_type=pl.DeviceIdType.MESH,
+        )
+
+    own_copy = pltpu.make_async_copy(piece_ref, whole_ref.at[mine], own_sem)
 
     @pl.when(pl.program_id(0) == 0)
     def _():
         pow_ref[...] = jnp.zeros_like(pow_ref)
+        barrier = pltpu.get_barrier_semaphore()
+
+        def greet(step, carry):
+            _, where = gather_peer(step, counts)
+            pl.semaphore_signal(barrier, inc=1, device_id=where, device_id_type=pl.DeviceIdType.MESH)
+            return carry
+
+        def send(step, carry):
+            to_peer(step).start()
+            return carry
+
+        lax.fori_loop(1, holders, greet, 0)
+        pl.semaphore_wait(barrier, holders - 1)
+        lax.fori_loop(1, holders, send, 0)
+        own_copy.start()
+
+    @pl.when(pl.program_id(0) == pl.num_programs(0) - 1)
+    def _():
+        def settle_copy(step, carry):
+            to_peer(step).wait()
+            return carry
+
+        lax.fori_loop(1, holders, settle_copy, 0)
+        own_copy.wait()
 
     ext[0:lead, :] = jnp.zeros((lead, ext.shape[1]), jnp.float32)
     ext[lead : 2 * lead, :] = wide(rim_ref[...])
-    gain = gain_ref[...]
+    gain = gain_ref[0:1, :]
     for at in range(0, rows, CHUNK):
         block = wide(hid_ref[at : at + CHUNK, :])
         ext[2 * lead + at : 2 * lead + at + CHUNK, :] = rounded(block * scale_ref[at : at + CHUNK, :] * gain)
@@ -109,7 +161,7 @@
     for at in range(0, rows, CHUNK):
         inner_rows(lead + at, CHUNK)
     q_taps = feature_rows(feat_ref, 0)
-    short = [taps_ref[lag : lag + 1, :] for lag in range(tap_count)]
+    short = tap_rows(taps_ref[...])
     for at in range(0, rows, CHUNK):
         queries = rounded(tap_sum(ext, 2 * lead + at, CHUNK, q_taps))
         filtered = tap_sum(inner, lead + at, CHUNK, short)
@@ -118,42 +170,112 @@
         pow_ref[at : at + CHUNK, :] += square_lanes(wide(result))
 
 
-def short_mixer(residual, rim, scale, gain_row, features, taps):
+def short_mixer(residual, rim, scale, gains, features, taps, piece):
     rows, channels = residual.shape
     lead = rim.shape[0]
+    counts = (lax.axis_size("seq"), lax.axis_size("fsdp"))
+    holders = counts[0] * counts[1]
     column = lambda i: (0, i)
     fixed = lambda i: (0, 0)
     return pl.pallas_call(
-        short_kernel,
+        functools.partial(short_kernel, counts),
         grid=(channels // WIDTH,),
         in_specs=[
             pl.BlockSpec((rows, WIDTH), column),
             pl.BlockSpec((lead, WIDTH), column),
             pl.BlockSpec((rows, 1), fixed),
-            pl.BlockSpec((1, WIDTH), column),
-            pl.BlockSpec((features.shape[0], WIDTH), column),
+            pl.BlockSpec((gains.shape[0], WIDTH), column),
+            pl.BlockSpec((1, *features.shape[1:3], WIDTH), lambda i: (0, 0, 0, i)),
             pl.BlockSpec((taps.shape[0], WIDTH), column),
-        ],
-        out_specs=[pl.BlockSpec((rows, WIDTH), column), pl.BlockSpec((rows, 128), fixed)],
+            pl.BlockSpec(memory_space=pl.ANY),
+        ],
+        out_specs=[
+            pl.BlockSpec((rows, WIDTH), column),
+            pl.BlockSpec((rows, 128), fixed),
+            pl.BlockSpec(memory_space=pl.ANY),
+        ],
         out_shape=[
             jax.ShapeDtypeStruct((rows, channels), jnp.bfloat16),
             jax.ShapeDtypeStruct((rows, 128), jnp.float32),
+            jax.ShapeDtypeStruct((holders, *piece.shape), piece.dtype),
         ],
         scratch_shapes=[
             pltpu.VMEM((2 * lead + rows, WIDTH), jnp.float32),
             pltpu.VMEM((lead + rows, WIDTH), jnp.float32),
-        ],
+            pltpu.SemaphoreType.DMA((holders,)),
+            pltpu.SemaphoreType.DMA((holders,)),
+            pltpu.SemaphoreType.DMA,
+        ],
+        compiler_params=pltpu.CompilerParams(collective_id=1, has_side_effects=True),
         name="short_mixer",
-    )(residual, rim, scale, gain_row, features, taps)
+    )(residual, rim, scale, gains, features, taps, piece)
 
 
 def long_kernel(
-    res_ref, rim_ref, scale_ref, gain_ref, feat_ref, taps_ref, fwd_ref, inv_ref,
-    out_ref, pow_ref, ext, inner, spec_u, spec_w, spec_y, filt,
+    count, res_ref, edge_ref, scale_ref, gain_ref, feat_ref, taps_ref, fwd_ref, inv_ref,
+    out_ref, pow_ref, ext, inner, spec_u, spec_w, spec_y, filt, rim, send_sem, recv_sem,
 ):
     rows = res_ref.shape[0]
     tap_count = taps_ref.shape[0]
-    lead = rim_ref.shape[0]
+    lead = rim.shape[1]
+    step = pl.program_id(0)
+    blocks = pl.num_programs(0)
+    me = lax.axis_index("seq")
+    sends, receives = me < count - 1, me > 0
+
+    def onward(block):
+        return pltpu.make_async_remote_copy(
+            src_ref=edge_ref.at[:, pl.ds(pl.multiple_of(block * WIDTH, WIDTH), WIDTH)],
+            dst_ref=rim.at[block],
+            send_sem=send_sem.at[block],
+            recv_sem=recv_sem.at[block],
+            device_id={"seq": lax.rem(me + 1, count)},
+            device_id_type=pl.DeviceIdType.MESH,
+        )
+
+    @pl.when(step == 0)
+    def _():
+        barrier = pltpu.get_barrier_semaphore()
+
+        @pl.when(receives)
+        def _():
+            pl.semaphore_signal(barrier, inc=1, device_id={"seq": me - 1}, device_id_type=pl.DeviceIdType.MESH)
+
+        @pl.when(sends)
+        def _():
+            pl.semaphore_signal(barrier, inc=1, device_id={"seq": me + 1}, device_id_type=pl.DeviceIdType.MESH)
+
+        between = jnp.logical_and(receives, sends)
+
+        @pl.when(between)
+        def _():
+            pl.semaphore_wait(barrier, 2)
+
+        @pl.when(jnp.logical_not(between))
+        def _():
+            pl.semaphore_wait(barrier, 1)
+
+        @pl.when(sends)
+        def _():
+            def send(block, carry):
+                onward(block).start()
+                return carry
+
+            lax.fori_loop(0, blocks, send, 0)
+
+    @pl.when(receives)
+    def _():
+        onward(step).wait_recv()
+        ext[0:lead, :] = wide(rim[step])
+
+    @pl.when(jnp.logical_not(receives))
+    def _():
+        ext[0:lead, :] = jnp.zeros((lead, ext.shape[1]), jnp.float32)
+
+    @pl.when(sends)
+    def _():
+        onward(step).wait_send()
+
     window = tap_count + rows
     half = window // 2
 
@@ -161,8 +283,7 @@
     def _():
         pow_ref[...] = jnp.zeros_like(pow_ref)
 
-    ext[0:lead, :] = wide(rim_ref[...])
-    gain = gain_ref[...]
+    gain = gain_ref[1:2, :]
     for at in range(0, rows, CHUNK):
         block = wide(res_ref[at : at + CHUNK, :])
         ext[lead + at : lead + at + CHUNK, :] = rounded(block * scale_ref[at : at + CHUNK, :] * gain)
@@ -213,23 +334,24 @@
         pow_ref[at : at + CHUNK, :] += square_lanes(wide(result))
 
 
-def long_mixer(residual, rim, scale, gain_row, features, taps):
+def long_mixer(residual, edge, scale, gains, features, taps):
     rows, channels = residual.shape
-    lead, tap_count = rim.shape[0], taps.shape[0]
+    lead, tap_count = edge.shape[0], taps.shape[0]
+    count, blocks = lax.axis_size("seq"), channels // WIDTH
     window = rows + tap_count
     forward, inverse = transform_pair(window, tap_count)
     column = lambda i: (0, i)
     fixed = lambda i: (0, 0)
     whole = lambda i: (0, 0, 0)
     return pl.pallas_call(
-        long_kernel,
+        functools.partial(long_kernel, count),
         grid=(channels // WIDTH,),
         in_specs=[
             pl.BlockSpec((rows, WIDTH), column),
-            pl.BlockSpec((lead, WIDTH), column),
+            pl.BlockSpec(memory_space=pl.ANY),
             pl.BlockSpec((rows, 1), fixed),
-            pl.BlockSpec((1, WIDTH), column),
-            pl.BlockSpec((features.shape[0], WIDTH), column),
+            pl.BlockSpec((gains.shape[0], WIDTH), column),
+            pl.BlockSpec((1, *features.shape[1:3], WIDTH), lambda i: (1, 0, 0, i)),
             pl.BlockSpec((tap_count, WIDTH), column),
             pl.BlockSpec(forward.shape, whole),
             pl.BlockSpec(inverse.shape, whole),
@@ -246,9 +368,13 @@
             pltpu.VMEM((window, WIDTH), jnp.float32),
             pltpu.VMEM((PARTS, window, WIDTH), jnp.bfloat16),
             pltpu.VMEM((rows, WIDTH), jnp.float32),
-        ],
+            pltpu.VMEM((blocks, lead, WIDTH), jnp.bfloat16),
+            pltpu.SemaphoreType.DMA((blocks,)),
+            pltpu.SemaphoreType.DMA((blocks,)),
+        ],
+        compiler_params=pltpu.CompilerParams(collective_id=2, has_side_effects=True),
         name="long_mixer",
-    )(residual, rim, scale, gain_row, features, taps, jnp.asarray(forward), jnp.asarray(inverse))
+    )(residual, edge, scale, gains, features, taps, jnp.asarray(forward), jnp.asarray(inverse))
 
 
 def row_scale(row_power):
@@ -313,22 +439,19 @@
     row_count = residual.shape[0]
     short_back = FEAT_TAPS + SE_TAPS - 2
     long_back = FEAT_TAPS + MR_TAPS - 2
-    long_lead = -(-long_back // 8) * 8
+    long_lead = -(-long_back // 16) * 16
     widened = residual.astype(jnp.float32)
     scale_one = row_scale(jnp.sum(widened * widened, axis=1))
     last = row_count - short_back
     rim_rows = passed_along(scaled_rows(residual[last:], scale_one[last:], norm_gain[0]), "seq", 1)
-    features = feature_taps.astype(jnp.float32).reshape(2, 3 * FEAT_TAPS, -1)
-    after_short, power_two = short_mixer(
-        residual, rim_rows, scale_one[:, None], norm_gain[0:1], features[0], short_taps.astype(jnp.float32)
+    after_short, power_two, taps_all = short_mixer(
+        residual, rim_rows, scale_one[:, None], norm_gain, feature_taps, short_taps, long_taps
     )
     scale_two = row_scale(jnp.sum(power_two, axis=1))
-    last = row_count - long_back
-    rim_long = passed_along(scaled_rows(after_short[last:], scale_two[last:], norm_gain[1]), "seq", 1)
-    rim_long = jnp.pad(rim_long, ((long_lead - long_back, 0), (0, 0)))
-    taps_all = lax.all_gather(long_taps, ("seq", "fsdp"), axis=0, tiled=True)
+    last = row_count - long_lead
+    edge_rows = scaled_rows(after_short[last:], scale_two[last:], norm_gain[1])
     after_long, power_three = long_mixer(
-        after_short, rim_long, scale_two[:, None], norm_gain[1:2], features[1], taps_all
+        after_short, edge_rows, scale_two[:, None], norm_gain, feature_taps, taps_all.reshape(MR_TAPS, -1)
     )
     final_norm = scaled_rows(after_long, row_scale(jnp.sum(power_three, axis=1)), norm_gain[2])
     row_contract = (((1,), (1,)), ((), ()))

time: 162 us -> 164 us (1.012)
  Pallas kernels: 59.3 us -> 115 us
  waiting for transfers between devices: 52.9 us -> 6.4 us
  starting transfers between devices: 9.39 us -> 6 us
  local copies, waits for them, and re-layouts: 6.24 us -> 3.25 us
    pallas_call x2, Pallas kernels: 52.5 us -> 102 us  [the longest x1 65.3 us: long_mixer(): pl.pallas_call(functools.partial(long_kernel, count), grid=(channels // W...]
    ppermute x2 -> x1, waiting for transfers between devices: 34.9 us -> 0.27 us  [passed_along(): return lax.ppermute(shard, axis, pairs)]
    all_gather x1, waiting for transfers between devices: 11.2 us -> 0.02 us  [shards(): lax.all_gather(head_weight, ('seq', 'fsdp'), axis=0, tiled=True)]
    pallas_call x1, Pallas kernels: 6.72 us -> 12.9 us  [spread(): pl.pallas_call(functools.partial(spread_kernel, count), out_shape=jax.Sha...]
    ppermute x2 -> x1, starting transfers between devices: 8.35 us -> 4.81 us  [passed_along(): return lax.ppermute(shard, axis, pairs)]
  transfers between devices with their start and end apart: 9 -> 7, of which waited for: 7 -> 6; matrix products, arithmetic and copies ran while one was open for 10% -> 8% of each run, Pallas kernels for 33% -> 62%
where the time goes in v2:
time: 164 us; the launch traced here: 163 us
  Pallas kernels  115 us (70%)
  between operations  16 us (10%)
  other arithmetic  13.5 us (8%)
  waiting for transfers between devices  6.4 us (4%)
  starting transfers between devices  6 us (4%)
  matrix products  3.51 us (2%)
  local copies, waits for them, and re-layouts  3.25 us (2%)
    pallas_call x1, Pallas kernels, long_mixer(): pl.pallas_call(functools.partial(long_kernel, count), grid=(channels // W...  65.3 us
    pallas_call x1, Pallas kernels, short_mixer(): pl.pallas_call(functools.partial(short_kernel, counts), grid=(channels //...  36.4 us
    pallas_call x1, Pallas kernels, spread(): pl.pallas_call(functools.partial(spread_kernel, count), out_shape=jax.Sha...  12.9 us
    convert_element_type x3, other arithmetic, settle(): return lax.optimization_barrier(tensor.astype(jnp.bfloat16))  5.89 us
    ppermute x1, starting transfers between devices, passed_along(): return lax.ppermute(shard, axis, pairs)  4.81 us
    dot_general x1, matrix products, shards(): lax.dot_general(final_norm, lax.all_gather(head_weight, ('seq', 'fsdp'),...  3.51 us
  transfers between devices with their start and end apart: 7, of which 6 were waited for; matrix products, arithmetic and copies ran while one was open for 8% of the time, Pallas kernels for 62%

profile of v2, /device:TPU:0, one launch (start us, length us, event | category | flops | bytes accessed | tf_op | source)
XLA Modules:
  0.0 163.3 jit_solution(15595965348198525618)
XLA Ops:
  7.2 0.0 copy-start
  7.2 0.0 copy-start.1
  7.2 0.0 copy-start.2
  7.2 0.0 all-gather.2.cloned.1.call-start
  7.2 0.7 all-gather.2.cloned.1.call-update
  7.9 2.1 %multiply_reduce_fusion = f32[256]{0:T(256)S(1)} fusion(bf16[1,256,4096]{2,1,0:T(8,128)(2,1)} %param.11), kind=kLoop, calls=%fused_computation.1 | loop fusion | flops 3145472 | bytes 2098176 | tf_op jit(solution)/shard_map/reduce_sum | solution.py:444
  10.0 0.6 collective-permute-start
  10.6 0.0 copy-done.1
  10.6 0.8 collective-permute-done
  11.4 0.1 slice.23
  11.5 0.9 fusion.1
  12.4 4.8 %collective-permute-start.1 = (bf16[8,4096]{1,0:T(8,128)(2,1)S(1)}, bf16[8,4096]{1,0:T(8,128)(2,1)S(1)}, u32[]{:S(2)}, u32[]{:S(2)}) collective-permute-start(bf16[8,4096]{1,0:T(8,128)(2,1)S(1)} %fusion.1), channel_id=1, source_target_pairs={{0,4},{4,8},{8,12},{1,5},{5,9},{9,13},{2,6},{6,10},{10,14},{3,7},{... | collective-permute-start | bytes 196616 | tf_op jit(solution)/shard_map/ppermute | solution.py:24
  17.2 0.0 copy-done.2
  17.2 0.8 copy.21.feat_ref
  18.0 0.8 copy.20.scale_ref
  18.8 0.3 collective-permute-done.1.rim_ref
  19.1 0.6 copy-done.3
  19.7 36.4 %short_mixer.1 = (bf16[256,4096]{1,0:T(8,128)(2,1)}, f32[256,128]{1,0:T(8,128)}, bf16[8,16,4096]{2,1,0:T(8,128)(2,1)}) custom-call(bf16[256,4096]{1,0:T(8,128)(2,1)} %bitcast.33, bf16[8,4096]{1,0:T(8,128)(2,1)} %copy-done.3, f32[256,1]{1,0:T(8,128)} %copy.20.scale_ref, f32[3,4096]{1,0:T(4,128)} %gain_ref.3, bf16[2,3,3,4096]{3,2,1,0:T(4,128)(2,1)} %copy.21.feat_ref, ...), custom_call_target="tpu_custom_call" | custom-call | tf_op jit(solution)/shard_map/short_mixer/pallas_call | solution.py:180
  56.1 1.0 reduce_sum.77
  57.1 0.1 collective-permute-start.2
  57.2 1.1 collective-permute-done.2
  58.4 0.1 slice.26
  58.5 2.7 %multiply_convert_fusion.1.edge_ref = bf16[144,4096]{1,0:T(8,128)(2,1)} fusion(f32[4096]{0:T(1024)S(1)} %bitcast.36, f32[144]{0:T(256)S(1)} %slice.26, bf16[256,4096]{1,0:T(8,128)(2,1)} %get-tuple-element.8.res_ref), kind=kLoop, calls=%fused_computation.2 | loop fusion | flops 2359296 | bytes 2376256 | tf_op jit(solution)/shard_map/convert_element_type | solution.py:28
  61.2 0.8 copy.22.scale_ref
  62.0 65.3 %long_mixer.1 = (bf16[256,4096]{1,0:T(8,128)(2,1)}, f32[256,128]{1,0:T(8,128)}) custom-call(bf16[256,4096]{1,0:T(8,128)(2,1)} %get-tuple-element.8.res_ref, bf16[144,4096]{1,0:T(8,128)(2,1)} %multiply_convert_fusion.1.edge_ref, f32[256,1]{1,0:T(8,128)} %copy.22.scale_ref, f32[3,4096]{1,0:T(4,128)} %gain_ref.3, bf16[2,3,3,4096]{3,2,1,0:T(4,128)(2,1)} %copy.21.feat_ref, ...), custom_call_target="tpu_custom_call" | custom-call | tf_op jit(solution)/shard_map/long_mixer/pallas_call | solution.py:346
  127.3 1.0 reduce_sum.78
  128.4 0.1 collective-permute-start.3
  128.4 1.1 collective-permute-done.3
  129.6 2.2 %multiply_convert_fusion = bf16[256,4096]{1,0:T(8,128)(2,1)S(1)} fusion(bf16[256,4096]{1,0:T(8,128)(2,1)} %get-tuple-element.11, f32[4096]{0:T(1024)S(1)} %bitcast.35, f32[256]{0:T(256)S(1)} %add_rsqrt_fusion), kind=kLoop, calls=%fused_computation | loop fusion | flops 4194304 | bytes 4211712 | tf_op jit(solution)/shard_map/convert_element_type | solution.py:28
  131.8 0.0 copy-start.4
  131.8 0.0 copy-start.5
  131.8 0.0 all-gather.2.cloned.1.call-done
  131.9 3.5 %fusion.8 = f32[256,512]{1,0:T(8,128)S(1)} fusion(bf16[256,4096]{1,0:T(8,128)(2,1)S(1)} %multiply_convert_fusion, bf16[512,4096]{1,0:T(8,128)(2,1)} %all-gather.2.cloned.1.call-done), kind=kOutput, calls=%fused_computation.30 | convolution fusion | flops 1073741824 | bytes 6815744 | tf_op jit(solution)/shard_map/dot_general | solution.py:458
  135.4 0.2 collective-permute-start.4
  135.7 0.0 copy-done
  135.7 1.4 collective-permute-done.4
  137.0 0.1 fusion.6
  137.1 0.2 exponential_reduce_fusion
  137.4 0.2 collective-permute-start.5
  137.6 1.0 collective-permute-done.5
  138.6 0.6 fusion.2.mine_ref
  139.2 12.9 %spread.1 = f32[4,2,128]{2,1,0:T(2,128)} custom-call(f32[2,128]{1,0:T(2,128)} %fusion.2.mine_ref), custom_call_target="tpu_custom_call" | custom-call | tf_op jit(solution)/shard_map/spread/pallas_call | solution.py:416
  152.0 0.0 copy-done.4
  152.1 0.9 select_reduce_fusion.1
  153.0 0.5 fusion.5
  153.5 0.0 copy-done.5
  153.5 0.6 fusion.4
  154.8 0.6 broadcast_select_fusion
  (8 shorter events, 0.1 us)
Async XLA Ops:
  7.2 128.5 %copy-start = (s32[1,256]{1,0:T(1,128)S(1)}, s32[1,256]{1,0:T(1,128)}, u32[]{:S(2)}) copy-start(s32[1,256]{1,0:T(1,128)} %param.12) | copy-start | bytes 3076
  7.2 3.4 %copy-start.1 = (f32[3,4096]{1,0:T(4,128)S(1)}, f32[3,4096]{1,0:T(4,128)}, u32[]{:S(2)}) copy-start(f32[3,4096]{1,0:T(4,128)} %gain_ref.3) | copy-start | bytes 147460
  7.2 10.0 %copy-start.2 = (bf16[2,3,3,4096]{3,0,2,1:T(2,128)(2,1)S(1)}, bf16[2,3,3,4096]{3,0,2,1:T(2,128)(2,1)}, u32[]{:S(2)}) copy-start(bf16[2,3,3,4096]{3,0,2,1:T(2,128)(2,1)} %param.16) | copy-start | bytes 442372
  7.2 124.7 %all-gather.2.cloned.1.call-start = ((), (), s32[]{:S(2)}) async-start(), calls=%async_computation | async-start | bytes 4718592 | tf_op jit(solution)/shard_map/all_gather | solution.py:460
  10.0 1.4 collective-permute-start
  12.4 6.7 %collective-permute-start.1 = (bf16[8,4096]{1,0:T(8,128)(2,1)S(1)}, bf16[8,4096]{1,0:T(8,128)(2,1)S(1)}, u32[]{:S(2)}, u32[]{:S(2)}) collective-permute-start(bf16[8,4096]{1,0:T(8,128)(2,1)S(1)} %fusion.1), channel_id=1, source_target_pairs={{0,4},{4,8},{8,12},{1,5},{5,9},{9,13},{2,6},{6,10},{10,14},{3,7},{... | collective-permute-start | bytes 196616 | tf_op jit(solution)/shard_map/ppermute | solution.py:24
  19.1 0.6 copy-start.3
  57.1 1.2 collective-permute-start.2
  128.4 1.2 collective-permute-start.3
  131.8 20.2 %copy-start.4 = (s32[1,64]{1,0:T(1,128)S(1)}, s32[1,64]{1,0:T(1,128)}, u32[]{:S(2)}) copy-start(s32[1,64]{1,0:T(1,128)} %param.13) | copy-start | bytes 772
  131.8 21.7 %copy-start.5 = (s32[1,64]{1,0:T(1,128)S(1)}, s32[1,64]{1,0:T(1,128)}, u32[]{:S(2)}) copy-start(s32[1,64]{1,0:T(1,128)} %param.14) | copy-start | bytes 772
  135.4 1.6 collective-permute-start.4
  137.4 1.2 collective-permute-start.5
Sparse Core Ops, SparseCore 0:
  10.1 114.2 all-gather.1

commit v3 on v2

--- a/solution.py
+++ b/solution.py
@@ -373,6 +373,7 @@
             pltpu.SemaphoreType.DMA((blocks,)),
         ],
         compiler_params=pltpu.CompilerParams(collective_id=2, has_side_effects=True),
+        cost_estimate=pl.CostEstimate(flops=12 * window * window * channels, bytes_accessed=8 * rows * channels, transcendentals=0),
         name="long_mixer",
     )(residual, edge, scale, gains, features, taps, jnp.asarray(forward), jnp.asarray(inverse))
 
@@ -450,16 +451,21 @@
     scale_two = row_scale(jnp.sum(power_two, axis=1))
     last = row_count - long_lead
     edge_rows = scaled_rows(after_short[last:], scale_two[last:], norm_gain[1])
+    part, parts = lax.axis_index("grp"), lax.axis_size("grp")
+    slab = head_weight.shape[0] // parts
+    own_slab = lax.dynamic_slice_in_dim(head_weight, part * slab, slab, 0)
+    head_own = lax.all_gather(own_slab, ("seq", "fsdp"), axis=0, tiled=True)
+    taps_all, head_own = lax.optimization_barrier((taps_all, head_own))
+    heads = [head_own]
+    for turn in range(1, parts):
+        heads.append(lax.ppermute(head_own, "grp", [(i, (i + turn) % parts) for i in range(parts)]))
     after_long, power_three = long_mixer(
         after_short, edge_rows, scale_two[:, None], norm_gain, feature_taps, taps_all.reshape(MR_TAPS, -1)
     )
     final_norm = scaled_rows(after_long, row_scale(jnp.sum(power_three, axis=1)), norm_gain[2])
     row_contract = (((1,), (1,)), ((), ()))
-    logits_part = lax.dot_general(
-        final_norm,
-        lax.all_gather(head_weight, ("seq", "fsdp"), axis=0, tiled=True),
-        row_contract,
-        preferred_element_type=jnp.float32,
+    logits_part = jnp.concatenate(
+        [lax.dot_general(final_norm, head, row_contract, preferred_element_type=jnp.float32) for head in heads], axis=1
     )
     core = lax.axis_index("tp")
     swap = [(0, 1), (1, 0)]
@@ -470,7 +476,11 @@
     row_peak = jnp.max(logits, axis=1, keepdims=True)
     log_total = jnp.log(jnp.sum(jnp.exp(logits - row_peak), axis=1)) + row_peak[:, 0]
     target_row = lax.dynamic_slice_in_dim(targets[0], core * half_rows, half_rows, 0)
-    vocab_ids = lax.broadcasted_iota(jnp.int32, logits.shape, 1)
+    column = lax.broadcasted_iota(jnp.int32, logits.shape, 1)
+    section = head_own.shape[0]
+    from_part = lax.rem(part + parts - column // section, parts)
+    within = lax.rem(column, section)
+    vocab_ids = (within // slab) * head_weight.shape[0] + from_part * slab + lax.rem(within, slab)
     chosen = jnp.sum(jnp.where(vocab_ids == target_row[:, None], logits, 0.0), axis=1)
     mine = chosen - log_total
     theirs = lax.ppermute(mine, "tp", swap)

time: 164 us -> 148 us (0.902)
  Pallas kernels: 115 us -> 79.5 us
  waiting for transfers between devices: 6.4 us -> 23.4 us
  matrix products: 3.51 us -> 1.48 us
  local copies, waits for them, and re-layouts: 3.25 us -> 4.94 us
    pallas_call x1, Pallas kernels: 65.3 us -> 42.3 us  [long_mixer(): pl.pallas_call(functools.partial(long_kernel, count), grid=(channels // W...]
    all_gather x1, waiting for transfers between devices: 0.02 us -> 17.7 us  [shards(): head_own = lax.all_gather(own_slab, ('seq', 'fsdp'), axis=0, tiled=True)]
    pallas_call x1, Pallas kernels: 36.4 us -> 29.5 us  [short_mixer(): pl.pallas_call(functools.partial(short_kernel, counts), grid=(channels //...]
    pallas_call x1, Pallas kernels: 12.9 us -> 7.7 us  [spread(): pl.pallas_call(functools.partial(spread_kernel, count), out_shape=jax.Sha...]
    dot_general x1 -> x2, matrix products: 3.51 us -> 1.48 us  [shards(): lax.dot_general(final_norm, head, row_contract, preferred_element_type=jn...]
  transfers between devices with their start and end apart: 7 -> 8, of which waited for: 6 -> 7; matrix products, arithmetic and copies ran while one was open for 8% -> 9% of each run, Pallas kernels for 62% -> 49%
where the time goes in v3:
time: 148 us; the launch traced here: 147 us
  Pallas kernels  79.5 us (54%)
  waiting for transfers between devices  23.4 us (16%)
  between operations  16 us (11%)
  other arithmetic  14.1 us (10%)
  starting transfers between devices  7.48 us (5%)
  local copies, waits for them, and re-layouts  4.94 us (3%)
  matrix products  1.48 us (1%)
    pallas_call x1, Pallas kernels, long_mixer(): pl.pallas_call(functools.partial(long_kernel, count), grid=(channels // W...  42.3 us
    pallas_call x1, Pallas kernels, short_mixer(): pl.pallas_call(functools.partial(short_kernel, counts), grid=(channels //...  29.5 us
    all_gather x1, waiting for transfers between devices, shards(): head_own = lax.all_gather(own_slab, ('seq', 'fsdp'), axis=0, tiled=True)  17.7 us
    pallas_call x1, Pallas kernels, spread(): pl.pallas_call(functools.partial(spread_kernel, count), out_shape=jax.Sha...  7.7 us
    convert_element_type x3, other arithmetic, settle(): return lax.optimization_barrier(tensor.astype(jnp.bfloat16))  5.96 us
    ppermute x1, starting transfers between devices, passed_along(): return lax.ppermute(shard, axis, pairs)  4.81 us
    ppermute x3, waiting for transfers between devices, row_scale(): other = lax.ppermute(row_power, 'tp', [(0, 1), (1, 0)])  3.04 us
  transfers between devices with their start and end apart: 8, of which 7 were waited for; matrix products, arithmetic and copies ran while one was open for 9% of the time, Pallas kernels for 49%

profile of v3, /device:TPU:0, one launch (start us, length us, event | category | flops | bytes accessed | tf_op | source)
XLA Modules:
  0.0 147.0 jit_solution(27704192665801747)
XLA Ops:
  7.2 0.0 copy-start
  7.2 0.0 copy-start.2
  7.2 0.0 all-gather.2.cloned.1.call-start
  7.3 1.0 copy-done
  8.2 0.7 constant_dynamic-slice_fusion
  8.9 0.0 all-gather.2.cloned.1.call-update
  8.9 2.1 %multiply_reduce_fusion = f32[256]{0:T(256)S(1)} fusion(bf16[1,256,4096]{2,1,0:T(8,128)(2,1)} %param.11), kind=kLoop, calls=%fused_computation.1 | loop fusion | flops 3145472 | bytes 2098176 | tf_op jit(solution)/shard_map/reduce_sum | solution.py:445
  11.0 0.6 collective-permute-start
  11.6 0.8 collective-permute-done
  12.4 0.1 slice.23
  12.5 0.9 fusion.9
  13.4 4.8 %collective-permute-start.1 = (bf16[8,4096]{1,0:T(8,128)(2,1)S(1)}, bf16[8,4096]{1,0:T(8,128)(2,1)S(1)}, u32[]{:S(2)}, u32[]{:S(2)}) collective-permute-start(bf16[8,4096]{1,0:T(8,128)(2,1)S(1)} %fusion.9), channel_id=1, source_target_pairs={{0,4},{4,8},{8,12},{1,5},{5,9},{9,13},{2,6},{6,10},{10,14},{3,7},{... | collective-permute-start | bytes 196616 | tf_op jit(solution)/shard_map/ppermute | solution.py:24
  18.2 0.8 copy.21.feat_ref
  19.1 0.8 copy.20.scale_ref
  19.9 0.3 collective-permute-done.1.rim_ref
  20.1 0.6 copy-done.4
  20.7 29.5 %short_mixer.1 = (bf16[256,4096]{1,0:T(8,128)(2,1)}, f32[256,128]{1,0:T(8,128)}, bf16[8,16,4096]{2,1,0:T(8,128)(2,1)}) custom-call(bf16[256,4096]{1,0:T(8,128)(2,1)} %bitcast.35, bf16[8,4096]{1,0:T(8,128)(2,1)} %copy-done.4, f32[256,1]{1,0:T(8,128)} %copy.20.scale_ref, f32[3,4096]{1,0:T(4,128)} %gain_ref.3, bf16[2,3,3,4096]{3,2,1,0:T(4,128)(2,1)} %copy.21.feat_ref, ...), custom_call_target="tpu_custom_call" | custom-call | tf_op jit(solution)/shard_map/short_mixer/pallas_call | solution.py:180
  50.3 1.0 reduce_sum.77
  51.3 0.1 collective-permute-start.2
  51.4 1.1 collective-permute-done.2
  52.6 0.1 slice.26
  52.6 2.7 %multiply_convert_fusion.1.edge_ref = bf16[144,4096]{1,0:T(8,128)(2,1)} fusion(f32[4096]{0:T(1024)S(1)} %bitcast.37, f32[144]{0:T(256)S(1)} %slice.26, bf16[256,4096]{1,0:T(8,128)(2,1)} %get-tuple-element.10.res_ref), kind=kLoop, calls=%fused_computation.2 | loop fusion | flops 2359296 | bytes 2376256 | tf_op jit(solution)/shard_map/convert_element_type | solution.py:28
  55.3 0.8 copy.22.scale_ref
  56.1 17.7 %all-gather.2.cloned.1.call-done = bf16[256,4096]{1,0:T(8,128)(2,1)} async-done(((bf16[32,4096]{1,0:T(8,128)(2,1)}), bf16[256,4096]{1,0:T(8,128)(2,1)}) %all-gather.2.cloned.1.call-update) | async-done | bytes 2097168 | tf_op jit(solution)/shard_map/all_gather | solution.py:457
  73.8 1.5 collective-permute-start.4
  75.3 42.3 %long_mixer.1 = (bf16[256,4096]{1,0:T(8,128)(2,1)}, f32[256,128]{1,0:T(8,128)}) custom-call(bf16[256,4096]{1,0:T(8,128)(2,1)} %get-tuple-element.10.res_ref, bf16[144,4096]{1,0:T(8,128)(2,1)} %multiply_convert_fusion.1.edge_ref, f32[256,1]{1,0:T(8,128)} %copy.22.scale_ref, f32[3,4096]{1,0:T(4,128)} %gain_ref.3, bf16[2,3,3,4096]{3,2,1,0:T(4,128)(2,1)} %copy.21.feat_ref, ...), custom_call_target="tpu_custom_call" | custom-call | flops 7247757312 | bytes 8388608 | tf_op jit(solution)/shard_map/long_mixer/pallas_call | solution.py:346
  117.6 1.0 reduce_sum.78
  118.6 0.1 collective-permute-start.3
  118.7 1.1 collective-permute-done.3
  119.9 2.4 %multiply_convert_fusion = bf16[256,4096]{1,0:T(8,128)(2,1)S(1)} fusion(bf16[256,4096]{1,0:T(8,128)(2,1)} %get-tuple-element.14, f32[4096]{0:T(1024)S(1)} %bitcast.36, f32[256]{0:T(256)S(1)} %add_rsqrt_fusion), kind=kLoop, calls=%fused_computation | loop fusion | flops 4194304 | bytes 4211712 | tf_op jit(solution)/shard_map/convert_element_type | solution.py:28
  122.2 0.7 fusion.22
  123.0 0.0 copy-start.7
  123.0 0.0 collective-permute-done.4
  123.0 0.7 fusion.23
  123.8 0.0 copy-start.5
  123.8 0.0 copy-start.6
  123.8 0.2 collective-permute-start.5
  124.1 1.4 collective-permute-done.5
  125.4 0.1 fusion.19
  125.5 0.7 exponential_reduce_fusion
  126.2 0.2 collective-permute-start.6
  126.5 1.0 collective-permute-done.6
  127.4 0.6 fusion.15.mine_ref
  128.0 7.7 %spread.1 = f32[4,2,128]{2,1,0:T(2,128)} custom-call(f32[2,128]{1,0:T(2,128)} %fusion.15.mine_ref), custom_call_target="tpu_custom_call" | custom-call | tf_op jit(solution)/shard_map/spread/pallas_call | solution.py:417
  135.7 0.9 select_reduce_fusion.1
  136.6 0.5 fusion.18
  137.2 0.6 fusion.17
  138.4 0.6 broadcast_select_fusion
  (20 shorter events, 0.1 us)
Async XLA Ops:
  7.2 1.0 copy-start
  7.2 4.4 %copy-start.2 = (f32[3,4096]{1,0:T(4,128)S(1)}, f32[3,4096]{1,0:T(4,128)}, u32[]{:S(2)}) copy-start(f32[3,4096]{1,0:T(4,128)} %gain_ref.3) | copy-start | bytes 147460
  7.2 11.0 %copy-start.3 = (bf16[2,3,3,4096]{3,0,2,1:T(2,128)(2,1)S(1)}, bf16[2,3,3,4096]{3,0,2,1:T(2,128)(2,1)}, u32[]{:S(2)}) copy-start(bf16[2,3,3,4096]{3,0,2,1:T(2,128)(2,1)} %param.16) | copy-start | bytes 442372
  7.2 66.6 %all-gather.2.cloned.1.call-start = ((), (), s32[]{:S(2)}) async-start(), calls=%async_computation | async-start | bytes 2359296 | tf_op jit(solution)/shard_map/all_gather | solution.py:457
  11.0 1.4 collective-permute-start
  13.4 6.7 %collective-permute-start.1 = (bf16[8,4096]{1,0:T(8,128)(2,1)S(1)}, bf16[8,4096]{1,0:T(8,128)(2,1)S(1)}, u32[]{:S(2)}, u32[]{:S(2)}) collective-permute-start(bf16[8,4096]{1,0:T(8,128)(2,1)S(1)} %fusion.9), channel_id=1, source_target_pairs={{0,4},{4,8},{8,12},{1,5},{5,9},{9,13},{2,6},{6,10},{10,14},{3,7},{... | collective-permute-start | bytes 196616 | tf_op jit(solution)/shard_map/ppermute | solution.py:24
  20.1 0.6 copy-start.4
  51.3 1.2 collective-permute-start.2
  73.8 49.2 %collective-permute-start.4 = (bf16[256,4096]{1,0:T(8,128)(2,1)}, bf16[256,4096]{1,0:T(8,128)(2,1)S(1)}, u32[]{:S(2)}, u32[]{:S(2)}) collective-permute-start(bf16[256,4096]{1,0:T(8,128)(2,1)} %all-gather.2.cloned.1.call-done), channel_id=1, source_target_pairs={{0,16},{16,0},{1,17},{17,1},{2,18},{18,2},{3,19},{19,3},{4,20},{20... | collective-permute-start | bytes 6291464 | tf_op jit(solution)/shard_map/ppermute | solution.py:461
  118.6 1.2 collective-permute-start.3
  119.9 2.4 %copy-start.1 = (bf16[256,4096]{1,0:T(8,128)(2,1)S(1)}, bf16[256,4096]{1,0:T(8,128)(2,1)}, u32[]{:S(2)}) copy-start(bf16[256,4096]{1,0:T(8,128)(2,1)} %all-gather.2.cloned.1.call-done) | copy-start | bytes 6291460
  123.0 1.1 copy-start.7
  123.8 12.0 %copy-start.5 = (s32[1,64]{1,0:T(1,128)S(1)}, s32[1,64]{1,0:T(1,128)}, u32[]{:S(2)}) copy-start(s32[1,64]{1,0:T(1,128)} %param.13) | copy-start | bytes 772
  123.8 13.4 %copy-start.6 = (s32[1,64]{1,0:T(1,128)S(1)}, s32[1,64]{1,0:T(1,128)}, u32[]{:S(2)}) copy-start(s32[1,64]{1,0:T(1,128)} %param.14) | copy-start | bytes 772
  123.8 1.6 %collective-permute-start.5 = (f32[128,512]{0,1:T(8,128)S(1)}, f32[128,512]{0,1:T(8,128)S(1)}, u32[]{:S(2)}, u32[]{:S(2)}) collective-permute-start(f32[128,512]{0,1:T(8,128)S(1)} %fusion.5), channel_id=1, source_target_pairs={{0,1},{1,0},{2,3},{3,2},{4,5},{5,4},{6,7},{7,6},{8,9},{9,8},{10,11... | collective-permute-start | bytes 786440 | tf_op jit(solution)/shard_map/ppermute | solution.py:475
  126.2 1.2 collective-permute-start.6
Sparse Core Ops, SparseCore 0:
  10.1 63.6 all-gather.1
